TPU v7x, 128 devices: a whole 4x4x4 slice. The times are simulated.
128 devices in a mesh: pb: 4 (over z_lo, core), col: 32 (over x, y, z_hi).
Axes of the slice: x: 4, y: 4, z: 4 (z_hi: 2, z_lo: 2; z = z_hi * 2 + z_lo), core: 2. Of those that a mesh axis runs over, the one named last changes fastest.
Arguments:
- queries: float32 [131072, 1024], P(('pb', 'col')), may hold values from -6 to 6
- corpus: float32 [2048, 1024], P('col'), may hold values from -6 to 6
- rotation: float32 [1024, 1024], replicated, may hold values from -0.1875 to 0.1875
- counts: int32 [32], replicated, may hold values from 1 to 64, 1024 in all
- teacher: bfloat16 [131072, 2048], P(('pb', 'col')), may hold values from -6 to 6
- shift_student: float32 [131072], P(('pb', 'col')), may hold values from 0 to 1.5
- shift_teacher: float32 [131072], P(('pb', 'col')), may hold values from 0 to 1.5
Outputs:
- grad_rotation: float32 [1024, 1024], P(('pb', 'col'))
Inputs may be any that keep to these rules, and one draw needn't show every extreme that they name: The counts sum to 1024; some index of col has all 64 slots live.
All inputs are finite; a program needn't handle non-finite values.
Results may differ from a plain program's by a relative error of at most 0.0018.
Values may be sent and summed in bfloat16 or wider, within the bound.
A program may use at most 128 MiB of HBM per device.

v0:
```python
import math

import jax
import jax.numpy as jnp
from jax import lax
from jax.sharding import PartitionSpec as P

code_sharp = 1.0


def make_weights(
    query_bits, codes, teach, live_rows, shift_student, shift_teacher, factor, live_total
):
    scores = factor * lax.dot_general(
        query_bits, codes, (((1,), (1,)), ((), ())), preferred_element_type=jnp.float32
    )
    student = jnp.exp(scores - shift_student[:, None])
    target = jnp.exp(teach.astype(jnp.float32) - shift_teacher[:, None])
    return (live_rows[None, :] * (student - target) / live_total).astype(jnp.bfloat16)


def per_device(queries, corpus, rotation, counts, teacher, shift_student, shift_teacher):
    highest = lax.Precision.HIGHEST
    query_rows, width = queries.shape
    slot_rows = corpus.shape[0]
    col_count = lax.axis_size("col")
    slot_total = slot_rows * col_count
    live_total = slot_total // 2
    factor = 2.5 / math.sqrt(width)
    query_code = jnp.tanh(
        code_sharp
        * jnp.dot(queries, rotation, precision=highest, preferred_element_type=jnp.float32)
    )
    query_bits = query_code.astype(jnp.bfloat16)
    corpus_code = jnp.tanh(
        code_sharp
        * jnp.dot(corpus, rotation, precision=highest, preferred_element_type=jnp.float32)
    )
    corpus_bits = corpus_code.astype(jnp.bfloat16)
    owners_all = jnp.arange(col_count, dtype=jnp.int32)
    piece = lax.all_gather(corpus_bits, "col", axis=0, tiled=True)
    count = piece.shape[0]
    index = jnp.arange(count, dtype=jnp.int32)
    owner = index // slot_rows
    onehot = owner[:, None] == owners_all[None, :]
    limit = jnp.sum(jnp.where(onehot, counts[None, :], 0), axis=1)
    live_rows = (index % slot_rows < limit).astype(jnp.float32)
    weights = make_weights(
        query_bits, piece, teacher, live_rows, shift_student, shift_teacher, factor, live_total
    )
    grad_acc = jnp.dot(weights, piece, preferred_element_type=jnp.float32)
    query_grad = factor * grad_acc
    corpus_grad = lax.psum_scatter(
        factor
        * lax.dot_general(
            weights, query_bits, (((0,), (0,)), ((), ())), preferred_element_type=jnp.float32
        ),
        "col",
        scatter_dimension=0,
        tiled=True,
    )
    query_local = (1.0 - query_code * query_code) * query_grad
    corpus_local = (1.0 - corpus_code * corpus_code) * corpus_grad
    partial_grad = lax.dot_general(
        queries,
        query_local,
        (((0,), (0,)), ((), ())),
        precision=highest,
        preferred_element_type=jnp.float32,
    )
    partial_grad = partial_grad + lax.dot_general(
        corpus,
        corpus_local,
        (((0,), (0,)), ((), ())),
        precision=highest,
        preferred_element_type=jnp.float32,
    )
    return lax.psum_scatter(
        code_sharp * partial_grad, ("pb", "col"), scatter_dimension=0, tiled=True
    )


def solution(mesh):
    in_specs = (
        P(("pb", "col"), None),
        P("col", None),
        P(),
        P(),
        P(("pb", "col"), None),
        P(("pb", "col")),
        P(("pb", "col")),
    )
    out_specs = P(("pb", "col"), None)
    return jax.shard_map(
        per_device, mesh=mesh, in_specs=in_specs, out_specs=out_specs, check_vma=False
    )
```

profile of v0, /device:TPU:0, one launch (start us, length us, event | category | flops | bytes accessed | tf_op | source)
XLA Modules:
  0.0 1002.3 jit_solution(12186698743966251235)
XLA Ops:
  6.5 0.0 copy-start
  6.5 0.0 all-gather.2.cloned.1.call-start
  6.5 0.9 copy-done
  7.5 5.5 fusion.22
  13.0 0.0 all-gather.2.cloned.1.call-update
  13.0 0.2 reduce-scatter.5.cloned.1.call-start
  13.2 0.0 copy-done.1
  13.2 0.1 select_reduce_fusion
  13.4 0.0 copy-start.3
  13.4 0.0 copy-start.4
  13.4 17.6 %fusion.23 = f32[1024,1024]{1,0:T(8,128)} fusion(f32[1024,1024]{1,0:T(8,128)} %param.7, f32[1024,1024]{1,0:T(8,128)} %param.9), kind=kOutput, calls=%fused_computation.35 | convolution fusion | flops 12884901888 | bytes 12582912 | tf_op jit(solution)/shard_map/dot_general | solution.py:32
  31.0 67.2 %all-gather.2.cloned.1.call-done = bf16[2048,1024]{1,0:T(8,128)(2,1)} async-done(((bf16[64,1024]{1,0:T(8,128)(2,1)}), bf16[2048,1024]{1,0:T(8,128)(2,1)}) %all-gather.2.cloned.1.call-update) | async-done | bytes 4194320 | tf_op jit(solution)/shard_map/all_gather | solution.py:41
  98.2 0.0 copy-done.3
  98.2 0.0 copy-done.4
  98.2 10.3 %multiply_convert_fusion = bf16[1024,2048]{1,0:T(8,128)(2,1)S(1)} fusion(bf16[1024,2048]{1,0:T(8,128)(2,1)} %param.11, bf16[2048,1024]{1,0:T(8,128)(2,1)} %all-gather.2.cloned.1.call-done, f32[1024]{0:T(1024)S(1)} %copy-done.3, f32[1024]{0:T(1024)S(1)} %copy-done.4, f32[2048]{0:T(1024)S(1)} %fusion.18, f32[1024,1024]{1,0:T(8,128)} %fusion.23), kind=kOutput, calls=%fused_computation | convolution fusion | flops 4312793088 | bytes 16793600 | tf_op jit(solution)/shard_map/dot_general | solution.py:14
  108.5 0.0 copy-start.7
  108.5 1.9 copy-done.7
  110.4 0.0 copy-done.5
  110.4 6.9 convolution_multiply_fusion
  117.3 0.0 reduce-scatter.5.cloned.1.call-update
  117.4 0.3 reduce-scatter.7.cloned.1.call-start
  117.6 0.0 copy-start.2
  117.7 0.0 copy-start.6
  117.7 7.7 fusion.24
  125.3 0.0 copy-done.2
  125.3 0.0 copy-done.6
  125.3 15.7 %fusion = f32[1024,1024]{1,0:T(8,128)} fusion(f32[1024,1024]{1,0:T(8,128)S(1)} %copy-done.2, f32[1024,1024]{1,0:T(8,128)S(1)} %fusion.24, f32[1024,1024]{1,0:T(8,128)S(1)} %copy-done.6), kind=kOutput, calls=%fused_computation.3 | convolution fusion | flops 12889096192 | bytes 16777216 | tf_op jit(solution)/shard_map/dot_general | solution.py:64
  141.1 179.3 %reduce-scatter.5.cloned.1.call-done = f32[64,1024]{1,0:T(8,128)} async-done(((f32[2048,1024]{1,0:T(8,128)}), f32[64,1024]{1,0:T(8,128)}) %reduce-scatter.5.cloned.1.call-update) | async-done | bytes 262160 | tf_op jit(solution)/shard_map/reduce_scatter | solution.py:53
  320.4 6.7 add_bitcast_fusion
  327.1 5.4 copy.11
  332.4 0.0 reduce-scatter.7.cloned.1.call-update
  332.4 663.3 %reduce-scatter.7.cloned.1.call-done = f32[8,1024]{1,0:T(8,128)} async-done(((f32[1024,1024]{1,0:T(8,128)}), f32[8,1024]{1,0:T(8,128)}) %reduce-scatter.7.cloned.1.call-update) | async-done | bytes 32784 | tf_op jit(solution)/shard_map/reduce_scatter | solution.py:78
  (4 shorter events, 0.0 us)
Async XLA Ops:
  6.5 1.0 copy-start
  6.5 6.7 copy-start.1
  6.5 91.6 %all-gather.2.cloned.1.call-start = ((), (), s32[]{:S(2)}) async-start(), calls=%async_computation.2 | async-start | bytes 4325376 | tf_op jit(solution)/shard_map/all_gather | solution.py:41
  13.0 307.4 %reduce-scatter.5.cloned.1.call-start = ((), (), s32[]{:S(2)}) async-start(), calls=%async_computation.3 | async-start | bytes 8650752 | tf_op jit(solution)/shard_map/reduce_scatter | solution.py:53
  13.4 84.8 %copy-start.3 = (f32[1024]{0:T(1024)S(1)}, f32[1024]{0:T(1024)}, u32[]{:S(2)}) copy-start(f32[1024]{0:T(1024)} %param.13) | copy-start | bytes 12292
  13.4 84.8 %copy-start.4 = (f32[1024]{0:T(1024)S(1)}, f32[1024]{0:T(1024)}, u32[]{:S(2)}) copy-start(f32[1024]{0:T(1024)} %param.12) | copy-start | bytes 12292
  98.2 12.2 %copy-start.5 = (f32[1024,1024]{1,0:T(8,128)S(1)}, f32[1024,1024]{1,0:T(8,128)}, u32[]{:S(2)}) copy-start(f32[1024,1024]{1,0:T(8,128)} %fusion.23) | copy-start | bytes 12582916
  108.5 1.9 copy-start.7
  117.4 878.4 %reduce-scatter.7.cloned.1.call-start = ((), (), s32[]{:S(2)}) async-start(), calls=%async_computation.4 | async-start | bytes 4227072 | tf_op jit(solution)/shard_map/reduce_scatter | solution.py:78
  117.6 7.7 copy-start.2
  117.7 7.7 copy-start.6
Sparse Core Ops, SparseCore 0:
  13.1 85.0 all-gather.1
  117.5 202.8 reduce-scatter.4
  332.6 663.1 reduce-scatter.6
where the time goes:
time: 1000 us
  waiting for transfers between devices  910 us (91%)
  matrix products  70.3 us (7%)
  between operations  13.2 us (1%)
    reduce_scatter x1, waiting for transfers between devices, per_device(): lax.psum_scatter(code_sharp * partial_grad, ('pb', 'col'), scatter_dimens...  663 us
    reduce_scatter x1, waiting for transfers between devices, per_device(): lax.psum_scatter(factor * lax.dot_general(weights, query_bits, (((0,), (0...  179 us
    all_gather x1, waiting for transfers between devices, per_device(): piece = lax.all_gather(corpus_bits, 'col', axis=0, tiled=True)  67.2 us
  transfers between devices with their start and end apart: 3, of which 3 were waited for; matrix products, arithmetic and copies ran while one was open for 4% of the time, Pallas kernels for 0%

commit v1 on v0

v1 whole, which is shorter than its diff:
```python
import functools
import math

import jax
import jax.numpy as jnp
from jax import lax
from jax.experimental import pallas as pl
from jax.experimental.pallas import tpu as pltpu
from jax.sharding import PartitionSpec as P

MESH = pl.DeviceIdType.MESH
F32 = jnp.float32
BF16 = jnp.bfloat16

RING = 4
ORDERS = ((0, 1, 2), (1, 2, 0), (2, 0, 1))
COLUMNS = ((0, 384), (384, 384), (768, 256))
COLOURS = len(ORDERS)


def split(value):
    high = value.astype(BF16)
    return high, (value - high.astype(F32)).astype(BF16)


def dot(a, b, dims):
    return lax.dot_general(a, b, (dims, ((), ())), preferred_element_type=F32)


NN = ((1,), (0,))
NT = ((1,), (1,))
TN = ((0,), (0,))


class Place:
    def __init__(self):
        pb, col = lax.axis_index("pb"), lax.axis_index("col")
        self.at = (col // 8, (col // 2) % 4, (col % 2) * 2 + pb // 2)
        self.core = pb % 2
        self.pb = pb

    def device(self, at, core):
        x, y, z = at
        return ((z % 2) * 2 + core, x * 8 + y * 2 + z // 2)

    def peer(self, axis, step):
        at = list(self.at)
        at[axis] = (at[axis] + step) % RING
        return at[axis], self.device(at, self.core)

    def partner(self):
        return self.device(self.at, 1 - self.core)


def remote(src, dst, send, recv, device):
    return pltpu.make_async_remote_copy(
        src_ref=src,
        dst_ref=dst,
        send_sem=send,
        recv_sem=recv,
        device_id=device,
        device_id_type=MESH,
    )


class Gather:
    def __init__(self, place, codes, send, recv, pair_send, pair_recv):
        self.place, self.codes = place, codes
        self.send, self.recv = send, recv
        self.pair_send, self.pair_recv = pair_send, pair_recv

    def region(self, colour, known, last=None):
        order, (start, width) = ORDERS[colour], COLUMNS[colour]
        index = list(self.place.at)
        for axis in order[:known]:
            index[axis] = slice(None)
        if last is not None:
            index[order[2]] = last
        return self.codes.at[
            index[0], index[1], index[2], self.place.core, :, start : start + width
        ]

    def copies(self, stage):
        for colour in range(COLOURS):
            part = self.region(colour, stage)
            for step in range(1, RING):
                slot = (colour * 3 + stage) * 3 + step - 1
                _, device = self.place.peer(ORDERS[colour][stage], step)
                yield remote(
                    part, part, self.send.at[slot], self.recv.at[slot], device
                )

    def start(self, stage):
        for copy in self.copies(stage):
            copy.start()

    def wait(self, stage):
        for copy in self.copies(stage):
            copy.wait()

    def pair(self, colour, step):
        source, _ = self.place.peer(ORDERS[colour][2], -step)
        part = self.region(colour, 2, source)
        slot = colour * RING + step
        return remote(
            part,
            part,
            self.pair_send.at[slot],
            self.pair_recv.at[slot],
            self.place.partner(),
        )

    def finish(self):
        for step in range(1, RING):
            for colour in range(COLOURS):
                slot = (colour * 3 + 2) * 3 + step - 1
                part = self.region(colour, 2)
                _, device = self.place.peer(ORDERS[colour][2], step)
                remote(
                    part, part, self.send.at[slot], self.recv.at[slot], device
                ).wait()
                self.pair(colour, step).start()
        for colour in range(COLOURS):
            for step in range(RING):
                self.pair(colour, step).wait()


class Scatter:
    def __init__(self, place, total, lands, send, recv):
        self.place, self.total, self.lands = place, total, lands
        self.send, self.recv = send, recv

    def copies(self, stage):
        for colour in range(COLOURS):
            order, (start, width) = ORDERS[colour], COLUMNS[colour]
            for step in range(1, RING):
                slot = (colour * 3 + stage) * 3 + step - 1
                index = [slice(None)] * 3
                for axis in order[:stage]:
                    index[axis] = self.place.at[axis]
                index[order[stage]], device = self.place.peer(order[stage], step)
                yield remote(
                    self.total.at[index[0], index[1], index[2], :, start : start + width],
                    self.lands[stage][colour].at[step - 1],
                    self.send.at[slot],
                    self.recv.at[slot],
                    device,
                )

    def start(self, stage):
        for copy in self.copies(stage):
            copy.start()

    def wait(self, stage):
        for copy in self.copies(stage):
            copy.wait()
        for colour in range(COLOURS):
            order, (start, width) = ORDERS[colour], COLUMNS[colour]
            land = self.lands[stage][colour]
            rest = sorted(order[stage + 1 :])

            def add(item, _):
                index = list(self.place.at)
                inner = [item // RING, item % RING][2 - len(rest) :]
                for axis, at in zip(rest, inner):
                    index[axis] = at
                value = self.total[
                    index[0], index[1], index[2], :, start : start + width
                ]
                for step in range(RING - 1):
                    value = value + land[(step, *inner)]
                self.total[index[0], index[1], index[2], :, start : start + width] = value
                return 0

            lax.fori_loop(0, RING ** len(rest), add, 0)


def kernel(
    factor,
    live_total,
    q_hbm,
    c_hbm,
    r_hbm,
    counts,
    t_hbm,
    shift_s_ref,
    shift_t_ref,
    out_ref,
    big_a,
    big_b,
    t_buf,
    c_buf,
    m_hi,
    m_lo,
    q_hi,
    q_lo,
    q_bits,
    d_q,
    d_c,
    codes,
    weights,
    shift_s,
    shift_t,
    total_c,
    total_g,
    *rest,
):
    lands_c, rest = (rest[0:3], rest[3:6], rest[6:9]), rest[9:]
    lands_g, rest = (rest[0:3], rest[3:6], rest[6:9]), rest[9:]
    (
        load,
        ag_send,
        ag_recv,
        agp_send,
        agp_recv,
        c_send,
        c_recv,
        cp_send,
        cp_recv,
        g_send,
        g_recv,
        gp_send,
        gp_recv,
    ) = rest

    place = Place()
    core = place.core
    mx, my, mz = place.at

    load_r = pltpu.make_async_copy(r_hbm, big_a, load.at[0])
    load_c = pltpu.make_async_copy(
        c_hbm.at[pl.ds(place.pb * 16, 16), :], c_buf, load.at[1]
    )
    load_q = pltpu.make_async_copy(q_hbm, big_b.at[0:2], load.at[2])
    load_t = pltpu.make_async_copy(t_hbm, t_buf, load.at[3])
    load_c.start()
    load_r.start()
    load_q.start()
    load_t.start()

    barrier = pltpu.get_barrier_semaphore()
    for axis in range(3):
        for step in range(1, RING):
            _, device = place.peer(axis, step)
            pl.semaphore_signal(barrier, inc=1, device_id=device, device_id_type=MESH)
    pl.semaphore_signal(
        barrier, inc=1, device_id=place.partner(), device_id_type=MESH
    )

    load_r.wait()
    for x in range(RING):

        def split_rotation(item, _):
            value = big_a[x, item // RING, item % RING].reshape(16, -1)
            high, low = split(value)
            rows = pl.ds(pl.multiple_of(256 * x + 16 * item, 16), 16)
            m_hi[rows, :] = high
            m_lo[rows, :] = low
            return 0

        lax.fori_loop(0, RING * RING, split_rotation, 0)

    load_c.wait()
    c_high, c_low = split(c_buf[...])
    c_both = jnp.concatenate([c_high, c_low], axis=0)
    for tile in range(4):
        cols = slice(256 * tile, 256 * tile + 256)
        both = dot(c_both, m_hi[:, cols], NN)
        code = jnp.tanh(both[:16] + both[16:] + dot(c_high, m_lo[:, cols], NN))
        d_c[:, cols] = 1.0 - code * code
        codes[mx, my, mz, core, :, cols] = code.astype(BF16)

    pl.semaphore_wait(barrier, 10)
    gather = Gather(place, codes, ag_send, ag_recv, agp_send, agp_recv)
    gather.start(0)

    load_q.wait()

    def query_code(block):
        def split_queries(item, _):
            at = block * 16 + item
            value = big_b[at // 32, (at // 8) % 4, (at // 2) % 4, at % 2]
            high, low = split(value)
            rows = pl.ds(pl.multiple_of(16 * at, 16), 16)
            q_hi[rows, :] = high
            q_lo[rows, :] = low
            return 0

        lax.fori_loop(0, 16, split_queries, 0)
        rows = slice(256 * block, 256 * block + 256)

        def tile_code(tile, _):
            cols = pl.ds(pl.multiple_of(256 * tile, 256), 256)
            high = q_hi[rows, :]
            value = (
                dot(high, m_hi[:, cols], NN)
                + dot(high, m_lo[:, cols], NN)
                + dot(q_lo[rows, :], m_hi[:, cols], NN)
            )
            code = jnp.tanh(value)
            d_q[rows, cols] = factor * (1.0 - code * code)
            q_bits[rows, cols] = code.astype(BF16)
            return 0

        lax.fori_loop(0, 4, tile_code, 0)

    query_code(0)
    gather.wait(0)
    gather.start(1)
    query_code(1)
    gather.wait(1)
    gather.start(2)
    for colour in range(COLOURS):
        gather.pair(colour, 0).start()
    query_code(2)
    query_code(3)

    shift_s[...] = jnp.broadcast_to(shift_s_ref[...], (128, 1024)).T
    shift_t[...] = jnp.broadcast_to(shift_t_ref[...], (128, 1024)).T
    load_t.wait()
    gather.finish()

    def weigh(item, _):
        block, half = item // 2, item % 2
        cols = pl.ds(pl.multiple_of(256 * block, 256), 256)
        rows = pl.ds(pl.multiple_of(512 * half, 512), 512)
        part = codes[block // 2, pl.ds(2 * (block % 2), 2)].reshape(256, -1)
        score = factor * dot(q_bits[rows, :], part, NT)
        down_s, down_t = shift_s[rows, :], shift_t[rows, :]
        student = jnp.exp(score - jnp.concatenate([down_s, down_s], axis=1))
        target = jnp.exp(
            t_buf[rows, cols].astype(F32) - jnp.concatenate([down_t, down_t], axis=1)
        )
        lane = lax.broadcasted_iota(jnp.int32, (1, 256), 1)
        limit = jnp.zeros((1, 256), jnp.int32)
        for slot in range(4):
            limit = jnp.where(lane // 64 == slot, counts[4 * block + slot], limit)
        live = jnp.where(lane % 64 < limit, 1.0 / live_total, 0.0)
        weights[rows, cols] = (live * (student - target)).astype(BF16)
        return 0

    lax.fori_loop(0, 16, weigh, 0)

    def pair_c(x):
        return remote(
            big_b.at[x, :, :, 1 - core],
            total_c.at[x],
            cp_send.at[x],
            cp_recv.at[x],
            place.partner(),
        )

    for x in range(RING):

        def corpus_grad(item, _):
            half, tile = item // 4, item % 4
            cols = pl.ds(pl.multiple_of(256 * tile, 256), 256)
            slots = pl.ds(pl.multiple_of(512 * x + 256 * half, 256), 256)
            part = dot(weights[:, slots], q_bits[:, cols], TN)
            big_b[x, pl.ds(2 * half, 2), :, :, :, cols] = part.reshape(2, 4, 2, 16, 256)
            return 0

        lax.fori_loop(0, 8, corpus_grad, 0)
        pair_c(x).start()

    def own_c(x):
        def add(item, _):
            at = (x, item // RING, item % RING)
            total_c[at] = total_c[at] + big_b[(*at, core)]
            return 0

        lax.fori_loop(0, RING * RING, add, 0)

    for x in range(RING):
        pair_c(x).wait()
        own_c(x)
    scatter_c = Scatter(place, total_c, lands_c, c_send, c_recv)
    scatter_c.start(0)

    def query_grad(item, _):
        half, tile = item // 4, item % 4
        cols = pl.ds(pl.multiple_of(256 * tile, 256), 256)
        rows = pl.ds(pl.multiple_of(512 * half, 512), 512)
        part = codes[:, :, :, :, :, cols].reshape(2048, 256)
        grad = d_q[rows, cols] * dot(weights[rows, :], part, NN)
        high, low = split(grad)
        m_hi[rows, cols] = high
        m_lo[rows, cols] = low
        return 0

    lax.fori_loop(0, 8, query_grad, 0)

    def rotation_grad(group):
        z_low, half = group // 2, group % 2
        acols = slice(256 * group, 256 * group + 256)

        def tile_grad(tile, _):
            cols = pl.ds(pl.multiple_of(256 * tile, 256), 256)
            high = q_hi[:, acols]
            value = (
                dot(high, m_hi[:, cols], TN)
                + dot(high, m_lo[:, cols], TN)
                + dot(q_lo[:, acols], m_hi[:, cols], TN)
            )
            for item in range(32):
                big_a[item // 8, (item // 2) % 4, 2 * (item % 2) + z_low, half, :, cols] = (
                    value[8 * item : 8 * item + 8]
                )
            return 0

        lax.fori_loop(0, 4, tile_grad, 0)

    rotation_grad(0)
    scatter_c.wait(0)
    scatter_c.start(1)
    rotation_grad(1)
    scatter_c.wait(1)
    scatter_c.start(2)
    rotation_grad(2)
    rotation_grad(3)
    scatter_c.wait(2)

    g_high, g_low = split(factor * d_c[...] * total_c[mx, my, mz])
    left = jnp.concatenate([c_high, c_high, c_low], axis=0)
    right = jnp.concatenate([g_high, g_low, g_high], axis=0)
    for group in range(4):
        z_low, half = group // 2, group % 2
        value = dot(left[:, 256 * group : 256 * group + 256], right, TN)
        for item in range(32):
            at = (item // 8, (item // 2) % 4, 2 * (item % 2) + z_low, half)
            big_a[at] = big_a[at] + value[8 * item : 8 * item + 8]

    def pair_g(x):
        return remote(
            big_a.at[x, :, :, 1 - core],
            total_g.at[x],
            gp_send.at[x],
            gp_recv.at[x],
            place.partner(),
        )

    for x in range(RING):
        pair_g(x).start()
    for x in range(RING):
        pair_g(x).wait()

        def add(item, _):
            at = (x, item // RING, item % RING)
            total_g[at] = total_g[at] + big_a[(*at, core)]
            return 0

        lax.fori_loop(0, RING * RING, add, 0)
    scatter_g = Scatter(place, total_g, lands_g, g_send, g_recv)
    for stage in range(3):
        scatter_g.start(stage)
        scatter_g.wait(stage)
    out_ref[...] = total_g[mx, my, mz]


def per_device(queries, corpus, rotation, counts, teacher, shift_student, shift_teacher):
    rows, width = queries.shape
    slots = teacher.shape[1]
    factor = 2.5 / math.sqrt(width)

    def lands(depth, dtype):
        return [
            pltpu.VMEM((RING - 1, *(RING,) * (2 - stage), depth, COLUMNS[colour][1]), dtype)
            for stage in range(3)
            for colour in range(COLOURS)
        ]

    dma = pltpu.SemaphoreType.DMA
    any_space = pl.BlockSpec(memory_space=pl.ANY)
    vmem = pl.BlockSpec(memory_space=pltpu.VMEM)
    smem = pl.BlockSpec(memory_space=pltpu.SMEM)
    return pl.pallas_call(
        functools.partial(kernel, factor, slots // 2),
        out_shape=jax.ShapeDtypeStruct((8, width), F32),
        in_specs=[any_space, any_space, any_space, smem, any_space, vmem, vmem],
        out_specs=vmem,
        scratch_shapes=[
            pltpu.VMEM((4, 4, 4, 2, 8, width), F32),
            pltpu.VMEM((4, 4, 4, 2, 16, width), F32),
            pltpu.VMEM((rows, slots), BF16),
            pltpu.VMEM((16, width), F32),
            pltpu.VMEM((width, width), BF16),
            pltpu.VMEM((width, width), BF16),
            pltpu.VMEM((rows, width), BF16),
            pltpu.VMEM((rows, width), BF16),
            pltpu.VMEM((rows, width), BF16),
            pltpu.VMEM((rows, width), F32),
            pltpu.VMEM((16, width), F32),
            pltpu.VMEM((4, 4, 4, 2, 16, width), BF16),
            pltpu.VMEM((rows, slots), BF16),
            pltpu.VMEM((rows, 128), F32),
            pltpu.VMEM((rows, 128), F32),
            pltpu.VMEM((4, 4, 4, 16, width), F32),
            pltpu.VMEM((4, 4, 4, 8, width), F32),
            *lands(16, F32),
            *lands(8, F32),
            dma((4,)),
            dma((27,)),
            dma((27,)),
            dma((12,)),
            dma((12,)),
            dma((27,)),
            dma((27,)),
            dma((4,)),
            dma((4,)),
            dma((27,)),
            dma((27,)),
            dma((4,)),
            dma((4,)),
        ],
        compiler_params=pltpu.CompilerParams(
            collective_id=0, has_side_effects=True, vmem_limit_bytes=67043328
        ),
    )(
        queries.reshape(2, 4, 4, 2, 16, width),
        corpus,
        rotation.reshape(4, 4, 4, 2, 8, width),
        counts,
        teacher,
        shift_student.reshape(1, rows),
        shift_teacher.reshape(1, rows),
    )


def solution(mesh):
    in_specs = (
        P(("pb", "col"), None),
        P("col", None),
        P(),
        P(),
        P(("pb", "col"), None),
        P(("pb", "col")),
        P(("pb", "col")),
    )
    return jax.shard_map(
        per_device,
        mesh=mesh,
        in_specs=in_specs,
        out_specs=P(("pb", "col"), None),
        check_vma=False,
    )
```

time: 1000 us -> 117 us (0.12)
  waiting for transfers between devices: 910 us -> 0 us
  Pallas kernels: 0 us -> 115 us
  matrix products: 70.3 us -> 0 us
  between operations: 13.2 us -> 0.01 us
    reduce_scatter x2 -> x0, waiting for transfers between devices: 843 us -> none  [the longest x1 663 us: per_device(): lax.psum_scatter(code_sharp * partial_grad, ('pb', 'col'), scatter_dimens...]
    pallas_call x0 -> x1, Pallas kernels: none -> 115 us  [per_device(): pl.pallas_call(functools.partial(kernel, factor, slots // 2), out_shape=j...]
    dot_general x7 -> x0, matrix products: 70.3 us -> none  [the longest x1 17.6 us: per_device(): jnp.dot(queries, rotation, precision=highest, preferred_element_type=jnp....]
    all_gather x1 -> x0, waiting for transfers between devices: 67.2 us -> none  [per_device(): piece = lax.all_gather(corpus_bits, 'col', axis=0, tiled=True)]
  transfers between devices with their start and end apart: 3 -> 0, of which waited for: 3 -> 0; matrix products, arithmetic and copies ran while one was open for 4% -> 0% of each run, Pallas kernels for 0% -> 0%
where the time goes in v1:
time: 117 us
  Pallas kernels  115 us (98%)
  local copies, waits for them, and re-layouts  1.38 us (1%)
    pallas_call x1, Pallas kernels, per_device(): pl.pallas_call(functools.partial(kernel, factor, slots // 2), out_shape=j...  115 us

profile of v1, /device:TPU:0, one launch (start us, length us, event | category | flops | bytes accessed | tf_op | source)
XLA Modules:
  0.0 116.6 jit_solution(4924536742317172402)
XLA Ops:
  0.0 115.2 %shard_map.73 = f32[8,1024]{1,0:T(8,128)} custom-call(f32[2,4,4,2,16,1024]{5,4,3,2,1,0:T(8,128)} %bitcast.4, f32[64,1024]{1,0:T(8,128)} %c_hbm.1, f32[4,4,4,2,8,1024]{5,4,3,2,1,0:T(8,128)} %bitcast.5, s32[32]{0:T(128)} %counts.1, bf16[1024,2048]{1,0:T(8,128)(2,1)} %t_hbm.1, f32[1,1024]{1,0:T(1,128)} %bitcast.6, f32[1,1024]{1,0:T(1,128)} %bitcast.7), custom_call_target="tpu_custom_call" | custom-call | tf_op jit(solution)/shard_map/pallas_call | solution.py:476
  115.2 1.4 %copy.9 = f32[8,1024]{1,0:T(8,128)} copy(f32[8,1024]{1,0:T(8,128)} %shard_map.73) | data formatting | bytes 65536

commit v2 on v1

--- a/solution.py
+++ b/solution.py
@@ -16,6 +16,9 @@
 ORDERS = ((0, 1, 2), (1, 2, 0), (2, 0, 1))
 COLUMNS = ((0, 384), (384, 384), (768, 256))
 COLOURS = len(ORDERS)
+
+LOW, HIGH = slice(0, RING // 2), slice(RING // 2, RING)
+PIECES = 6
 
 
 def split(value):
@@ -69,11 +72,13 @@
         self.send, self.recv = send, recv
         self.pair_send, self.pair_recv = pair_send, pair_recv
 
-    def region(self, colour, known, last=None):
+    def region(self, colour, known, last=None, half=slice(None)):
         order, (start, width) = ORDERS[colour], COLUMNS[colour]
         index = list(self.place.at)
         for axis in order[:known]:
             index[axis] = slice(None)
+        if known == 2:
+            index[min(order[:2])] = half
         if last is not None:
             index[order[2]] = last
         return self.codes.at[
@@ -84,7 +89,7 @@
         for colour in range(COLOURS):
             part = self.region(colour, stage)
             for step in range(1, RING):
-                slot = (colour * 3 + stage) * 3 + step - 1
+                slot = (colour * 3 + stage) * PIECES + step - 1
                 _, device = self.place.peer(ORDERS[colour][stage], step)
                 yield remote(
                     part, part, self.send.at[slot], self.recv.at[slot], device
@@ -110,16 +115,38 @@
             self.place.partner(),
         )
 
+    def ring(self, colour, piece):
+        axis = ORDERS[colour][2]
+        up = piece in (0, 1, 4)
+        far, device = self.place.peer(axis, 1 if up else -1)
+        source = self.place.at[axis]
+        if piece > 3:
+            source, _ = self.place.peer(axis, -1 if up else 1)
+        half = (LOW, HIGH, HIGH, LOW, LOW, HIGH)[piece]
+        part = self.region(colour, 2, source, half)
+        slot = (colour * 3 + 2) * PIECES + piece
+        return remote(part, part, self.send.at[slot], self.recv.at[slot], device)
+
+    def start_ring(self):
+        for piece in (0, 2, 1, 3):
+            for colour in range(COLOURS):
+                self.ring(colour, piece).start()
+
+    def relay(self):
+        for piece in (0, 2):
+            for colour in range(COLOURS):
+                self.ring(colour, piece).wait()
+                self.ring(colour, 4 + piece // 2).start()
+
     def finish(self):
-        for step in range(1, RING):
+        for piece, step in ((1, 1), (3, 3)):
             for colour in range(COLOURS):
-                slot = (colour * 3 + 2) * 3 + step - 1
-                part = self.region(colour, 2)
-                _, device = self.place.peer(ORDERS[colour][2], step)
-                remote(
-                    part, part, self.send.at[slot], self.recv.at[slot], device
-                ).wait()
+                self.ring(colour, piece).wait()
                 self.pair(colour, step).start()
+        for colour in range(COLOURS):
+            self.ring(colour, 4).wait()
+            self.ring(colour, 5).wait()
+            self.pair(colour, 2).start()
         for colour in range(COLOURS):
             for step in range(RING):
                 self.pair(colour, step).wait()
@@ -130,11 +157,68 @@
         self.place, self.total, self.lands = place, total, lands
         self.send, self.recv = send, recv
 
+    def block(self, colour, at):
+        (start, width) = COLUMNS[colour]
+        index = [slice(None)] * 3
+        index[ORDERS[colour][0]] = at
+        return self.total.at[index[0], index[1], index[2], :, start : start + width]
+
+    def ring(self, colour, piece):
+        axis = ORDERS[colour][0]
+        up = piece % 2 == 0
+        at, device = self.place.peer(axis, 1 if up else -1)
+        if piece < 2:
+            at, _ = self.place.peer(axis, 2)
+        half = (LOW, HIGH, HIGH, LOW, LOW, HIGH)[piece]
+        land = self.lands[0][colour].at[2 if piece < 2 else piece % 2]
+        slot = colour * 3 * PIECES + piece
+        return remote(
+            self.block(colour, at).at[half],
+            land.at[half],
+            self.send.at[slot],
+            self.recv.at[slot],
+            device,
+        )
+
+    def start_ring(self):
+        for piece in range(4):
+            for colour in range(COLOURS):
+                self.ring(colour, piece).start()
+
+    def relay(self):
+        for piece in range(2):
+            for colour in range(COLOURS):
+                axis = ORDERS[colour][0]
+                self.ring(colour, piece).wait()
+                at, _ = self.place.peer(axis, 1 if piece == 0 else -1)
+                block, land = self.block(colour, at), self.lands[0][colour]
+
+                def add(item, _):
+                    inner = (piece * 2 + item // RING, item % RING)
+                    block[inner] = block[inner] + land[(2, *inner)]
+                    return 0
+
+                lax.fori_loop(0, 2 * RING, add, 0)
+                self.ring(colour, 4 + piece).start()
+
+    def finish_ring(self):
+        for colour in range(COLOURS):
+            for piece in range(2, PIECES):
+                self.ring(colour, piece).wait()
+            block, land = self.block(colour, self.place.at[ORDERS[colour][0]]), self.lands[0][colour]
+
+            def add(item, _):
+                inner = (item // RING, item % RING)
+                block[inner] = block[inner] + land[(0, *inner)] + land[(1, *inner)]
+                return 0
+
+            lax.fori_loop(0, RING * RING, add, 0)
+
     def copies(self, stage):
         for colour in range(COLOURS):
             order, (start, width) = ORDERS[colour], COLUMNS[colour]
             for step in range(1, RING):
-                slot = (colour * 3 + stage) * 3 + step - 1
+                slot = (colour * 3 + stage) * PIECES + step - 1
                 index = [slice(None)] * 3
                 for axis in order[:stage]:
                     index[axis] = self.place.at[axis]
@@ -203,6 +287,7 @@
     shift_t,
     total_c,
     total_g,
+    turned,
     *rest,
 ):
     lands_c, rest = (rest[0:3], rest[3:6], rest[6:9]), rest[9:]
@@ -309,10 +394,11 @@
     gather.start(1)
     query_code(1)
     gather.wait(1)
-    gather.start(2)
+    gather.start_ring()
     for colour in range(COLOURS):
         gather.pair(colour, 0).start()
     query_code(2)
+    gather.relay()
     query_code(3)
 
     shift_s[...] = jnp.broadcast_to(shift_s_ref[...], (128, 1024)).T
@@ -350,18 +436,19 @@
             place.partner(),
         )
 
-    for x in range(RING):
-
-        def corpus_grad(item, _):
-            half, tile = item // 4, item % 4
+    for group in range(8):
+        turned[0:256, :] = weights[:, 256 * group : 256 * group + 256].T
+
+        def corpus_grad(tile, _):
             cols = pl.ds(pl.multiple_of(256 * tile, 256), 256)
-            slots = pl.ds(pl.multiple_of(512 * x + 256 * half, 256), 256)
-            part = dot(weights[:, slots], q_bits[:, cols], TN)
-            big_b[x, pl.ds(2 * half, 2), :, :, :, cols] = part.reshape(2, 4, 2, 16, 256)
+            part = dot(turned[0:256, :], q_bits[:, cols], NN)
+            half = slice(2 * (group % 2), 2 * (group % 2) + 2)
+            big_b[group // 2, half, :, :, :, cols] = part.reshape(2, 4, 2, 16, 256)
             return 0
 
-        lax.fori_loop(0, 8, corpus_grad, 0)
-        pair_c(x).start()
+        lax.fori_loop(0, 4, corpus_grad, 0)
+        if group % 2:
+            pair_c(group // 2).start()
 
     def own_c(x):
         def add(item, _):
@@ -375,7 +462,7 @@
         pair_c(x).wait()
         own_c(x)
     scatter_c = Scatter(place, total_c, lands_c, c_send, c_recv)
-    scatter_c.start(0)
+    scatter_c.start_ring()
 
     def query_grad(item, _):
         half, tile = item // 4, item % 4
@@ -393,15 +480,13 @@
     def rotation_grad(group):
         z_low, half = group // 2, group % 2
         acols = slice(256 * group, 256 * group + 256)
+        turned[0:256, :] = q_hi[:, acols].T
+        turned[256:512, :] = q_lo[:, acols].T
 
         def tile_grad(tile, _):
             cols = pl.ds(pl.multiple_of(256 * tile, 256), 256)
-            high = q_hi[:, acols]
-            value = (
-                dot(high, m_hi[:, cols], TN)
-                + dot(high, m_lo[:, cols], TN)
-                + dot(q_lo[:, acols], m_hi[:, cols], TN)
-            )
+            both = dot(turned[...], m_hi[:, cols], NN)
+            value = both[:256] + both[256:] + dot(turned[0:256, :], m_lo[:, cols], NN)
             for item in range(32):
                 big_a[item // 8, (item // 2) % 4, 2 * (item % 2) + z_low, half, :, cols] = (
                     value[8 * item : 8 * item + 8]
@@ -410,14 +495,15 @@
 
         lax.fori_loop(0, 4, tile_grad, 0)
 
+    scatter_c.relay()
     rotation_grad(0)
-    scatter_c.wait(0)
+    rotation_grad(1)
+    rotation_grad(2)
+    scatter_c.finish_ring()
     scatter_c.start(1)
-    rotation_grad(1)
+    rotation_grad(3)
     scatter_c.wait(1)
     scatter_c.start(2)
-    rotation_grad(2)
-    rotation_grad(3)
     scatter_c.wait(2)
 
     g_high, g_low = split(factor * d_c[...] * total_c[mx, my, mz])
@@ -451,7 +537,10 @@
 
         lax.fori_loop(0, RING * RING, add, 0)
     scatter_g = Scatter(place, total_g, lands_g, g_send, g_recv)
-    for stage in range(3):
+    scatter_g.start_ring()
+    scatter_g.relay()
+    scatter_g.finish_ring()
+    for stage in (1, 2):
         scatter_g.start(stage)
         scatter_g.wait(stage)
     out_ref[...] = total_g[mx, my, mz]
@@ -496,19 +585,20 @@
             pltpu.VMEM((rows, 128), F32),
             pltpu.VMEM((4, 4, 4, 16, width), F32),
             pltpu.VMEM((4, 4, 4, 8, width), F32),
+            pltpu.VMEM((512, rows), BF16),
             *lands(16, F32),
             *lands(8, F32),
             dma((4,)),
-            dma((27,)),
-            dma((27,)),
+            dma((54,)),
+            dma((54,)),
             dma((12,)),
             dma((12,)),
-            dma((27,)),
-            dma((27,)),
+            dma((54,)),
+            dma((54,)),
             dma((4,)),
             dma((4,)),
-            dma((27,)),
-            dma((27,)),
+            dma((54,)),
+            dma((54,)),
             dma((4,)),
             dma((4,)),
         ],

time: 117 us -> 107 us (0.915)
  Pallas kernels: 115 us -> 105 us
    pallas_call x1, Pallas kernels: 115 us -> 105 us  [per_device(): pl.pallas_call(functools.partial(kernel, factor, slots // 2), out_shape=j...]
where the time goes in v2:
time: 107 us
  Pallas kernels  105 us (98%)
  local copies, waits for them, and re-layouts  1.38 us (1%)
    pallas_call x1, Pallas kernels, per_device(): pl.pallas_call(functools.partial(kernel, factor, slots // 2), out_shape=j...  105 us

profile of v2, /device:TPU:0, one launch (start us, length us, event | category | flops | bytes accessed | tf_op | source)
XLA Modules:
  0.0 106.8 jit_solution(969876667824280914)
XLA Ops:
  0.0 105.5 %shard_map.73 = f32[8,1024]{1,0:T(8,128)} custom-call(f32[2,4,4,2,16,1024]{5,4,3,2,1,0:T(8,128)} %bitcast.4, f32[64,1024]{1,0:T(8,128)} %c_hbm.1, f32[4,4,4,2,8,1024]{5,4,3,2,1,0:T(8,128)} %bitcast.5, s32[32]{0:T(128)} %counts.1, bf16[1024,2048]{1,0:T(8,128)(2,1)} %t_hbm.1, f32[1,1024]{1,0:T(1,128)} %bitcast.6, f32[1,1024]{1,0:T(1,128)} %bitcast.7), custom_call_target="tpu_custom_call" | custom-call | tf_op jit(solution)/shard_map/pallas_call | solution.py:565
  105.5 1.4 %copy.9 = f32[8,1024]{1,0:T(8,128)} copy(f32[8,1024]{1,0:T(8,128)} %shard_map.73) | data formatting | bytes 65536

commit v3 on v2

--- a/solution.py
+++ b/solution.py
@@ -153,15 +153,15 @@
 
 
 class Scatter:
-    def __init__(self, place, total, lands, send, recv):
-        self.place, self.total, self.lands = place, total, lands
+    def __init__(self, place, total, sent, lands, send, recv):
+        self.place, self.total, self.sent, self.lands = place, total, sent, lands
         self.send, self.recv = send, recv
 
-    def block(self, colour, at):
-        (start, width) = COLUMNS[colour]
+    def block(self, ref, colour, at):
+        start, width = COLUMNS[colour]
         index = [slice(None)] * 3
         index[ORDERS[colour][0]] = at
-        return self.total.at[index[0], index[1], index[2], :, start : start + width]
+        return ref.at[index[0], index[1], index[2], :, start : start + width]
 
     def ring(self, colour, piece):
         axis = ORDERS[colour][0]
@@ -173,7 +173,7 @@
         land = self.lands[0][colour].at[2 if piece < 2 else piece % 2]
         slot = colour * 3 * PIECES + piece
         return remote(
-            self.block(colour, at).at[half],
+            self.block(self.sent, colour, at).at[half],
             land.at[half],
             self.send.at[slot],
             self.recv.at[slot],
@@ -191,11 +191,13 @@
                 axis = ORDERS[colour][0]
                 self.ring(colour, piece).wait()
                 at, _ = self.place.peer(axis, 1 if piece == 0 else -1)
-                block, land = self.block(colour, at), self.lands[0][colour]
+                block, land = self.block(self.total, colour, at), self.lands[0][colour]
+                sent = self.block(self.sent, colour, at)
 
                 def add(item, _):
                     inner = (piece * 2 + item // RING, item % RING)
-                    block[inner] = block[inner] + land[(2, *inner)]
+                    value = block[inner] + land[(2, *inner)].astype(F32)
+                    sent[inner] = value.astype(sent.dtype)
                     return 0
 
                 lax.fori_loop(0, 2 * RING, add, 0)
@@ -205,11 +207,13 @@
         for colour in range(COLOURS):
             for piece in range(2, PIECES):
                 self.ring(colour, piece).wait()
-            block, land = self.block(colour, self.place.at[ORDERS[colour][0]]), self.lands[0][colour]
+            at = self.place.at[ORDERS[colour][0]]
+            block, land = self.block(self.total, colour, at), self.lands[0][colour]
 
             def add(item, _):
                 inner = (item // RING, item % RING)
-                block[inner] = block[inner] + land[(0, *inner)] + land[(1, *inner)]
+                first, second = land[(0, *inner)], land[(1, *inner)]
+                block[inner] = block[inner] + first.astype(F32) + second.astype(F32)
                 return 0
 
             lax.fori_loop(0, RING * RING, add, 0)
@@ -288,6 +292,10 @@
     total_c,
     total_g,
     turned,
+    sent_c,
+    slopes,
+    c_left,
+    c_right,
     *rest,
 ):
     lands_c, rest = (rest[0:3], rest[3:6], rest[6:9]), rest[9:]
@@ -306,6 +314,8 @@
         g_recv,
         gp_send,
         gp_recv,
+        swap_send,
+        swap_recv,
     ) = rest
 
     place = Place()
@@ -314,7 +324,7 @@
 
     load_r = pltpu.make_async_copy(r_hbm, big_a, load.at[0])
     load_c = pltpu.make_async_copy(
-        c_hbm.at[pl.ds(place.pb * 16, 16), :], c_buf, load.at[1]
+        c_hbm.at[pl.ds((place.pb // 2) * 32, 32), :], c_buf, load.at[1]
     )
     load_q = pltpu.make_async_copy(q_hbm, big_b.at[0:2], load.at[2])
     load_t = pltpu.make_async_copy(t_hbm, t_buf, load.at[3])
@@ -347,6 +357,8 @@
 
     load_c.wait()
     c_high, c_low = split(c_buf[...])
+    c_left[...] = jnp.concatenate([c_high, c_high, c_low], axis=0)
+    c_high, c_low = split(c_buf[pl.ds(pl.multiple_of(16 * core, 16), 16), :])
     c_both = jnp.concatenate([c_high, c_low], axis=0)
     for tile in range(4):
         cols = slice(256 * tile, 256 * tile + 256)
@@ -361,9 +373,9 @@
 
     load_q.wait()
 
-    def query_code(block):
+    def query_code(block, first):
         def split_queries(item, _):
-            at = block * 16 + item
+            at = block * 32 + item
             value = big_b[at // 32, (at // 8) % 4, (at // 2) % 4, at % 2]
             high, low = split(value)
             rows = pl.ds(pl.multiple_of(16 * at, 16), 16)
@@ -371,35 +383,36 @@
             q_lo[rows, :] = low
             return 0
 
-        lax.fori_loop(0, 16, split_queries, 0)
-        rows = slice(256 * block, 256 * block + 256)
+        if first == 0:
+            lax.fori_loop(0, 32, split_queries, 0)
+        rows = slice(512 * block, 512 * block + 512)
 
         def tile_code(tile, _):
             cols = pl.ds(pl.multiple_of(256 * tile, 256), 256)
             high = q_hi[rows, :]
             value = (
                 dot(high, m_hi[:, cols], NN)
+                + dot(q_lo[rows, :], m_hi[:, cols], NN)
                 + dot(high, m_lo[:, cols], NN)
-                + dot(q_lo[rows, :], m_hi[:, cols], NN)
             )
             code = jnp.tanh(value)
             d_q[rows, cols] = factor * (1.0 - code * code)
             q_bits[rows, cols] = code.astype(BF16)
             return 0
 
-        lax.fori_loop(0, 4, tile_code, 0)
-
-    query_code(0)
+        lax.fori_loop(first, first + 2, tile_code, 0)
+
+    query_code(0, 0)
     gather.wait(0)
     gather.start(1)
-    query_code(1)
+    query_code(0, 2)
     gather.wait(1)
     gather.start_ring()
     for colour in range(COLOURS):
         gather.pair(colour, 0).start()
-    query_code(2)
+    query_code(1, 0)
     gather.relay()
-    query_code(3)
+    query_code(1, 2)
 
     shift_s[...] = jnp.broadcast_to(shift_s_ref[...], (128, 1024)).T
     shift_t[...] = jnp.broadcast_to(shift_t_ref[...], (128, 1024)).T
@@ -436,24 +449,24 @@
             place.partner(),
         )
 
-    for group in range(8):
-        turned[0:256, :] = weights[:, 256 * group : 256 * group + 256].T
+    for x in range(RING):
+        turned[0:512, :] = weights[:, 512 * x : 512 * x + 512].T
 
         def corpus_grad(tile, _):
             cols = pl.ds(pl.multiple_of(256 * tile, 256), 256)
-            part = dot(turned[0:256, :], q_bits[:, cols], NN)
-            half = slice(2 * (group % 2), 2 * (group % 2) + 2)
-            big_b[group // 2, half, :, :, :, cols] = part.reshape(2, 4, 2, 16, 256)
+            part = dot(turned[0:512, :], q_bits[:, cols], NN)
+            big_b[x, :, :, :, :, cols] = part.reshape(4, 4, 2, 16, 256)
             return 0
 
         lax.fori_loop(0, 4, corpus_grad, 0)
-        if group % 2:
-            pair_c(group // 2).start()
+        pair_c(x).start()
 
     def own_c(x):
         def add(item, _):
             at = (x, item // RING, item % RING)
-            total_c[at] = total_c[at] + big_b[(*at, core)]
+            value = total_c[at] + big_b[(*at, core)]
+            total_c[at] = value
+            sent_c[at] = value.astype(BF16)
             return 0
 
         lax.fori_loop(0, RING * RING, add, 0)
@@ -461,7 +474,7 @@
     for x in range(RING):
         pair_c(x).wait()
         own_c(x)
-    scatter_c = Scatter(place, total_c, lands_c, c_send, c_recv)
+    scatter_c = Scatter(place, total_c, sent_c, lands_c, c_send, c_recv)
     scatter_c.start_ring()
 
     def query_grad(item, _):
@@ -477,44 +490,32 @@
 
     lax.fori_loop(0, 8, query_grad, 0)
 
-    def rotation_grad(group):
-        z_low, half = group // 2, group % 2
-        acols = slice(256 * group, 256 * group + 256)
-        turned[0:256, :] = q_hi[:, acols].T
-        turned[256:512, :] = q_lo[:, acols].T
-
+    def group_cols(z_low, half):
+        return pl.ds(pl.multiple_of(256 * (2 * z_low + half), 256), 256)
+
+    def turn(half):
+        for z_low in range(2):
+            rows = slice(256 * z_low, 256 * z_low + 256)
+            turned[rows, :] = q_hi[:, group_cols(z_low, half)].T
+            rows = slice(512 + 256 * z_low, 512 + 256 * z_low + 256)
+            turned[rows, :] = q_lo[:, group_cols(z_low, half)].T
+
+    def rotation_grad(half, first):
         def tile_grad(tile, _):
             cols = pl.ds(pl.multiple_of(256 * tile, 256), 256)
-            both = dot(turned[...], m_hi[:, cols], NN)
-            value = both[:256] + both[256:] + dot(turned[0:256, :], m_lo[:, cols], NN)
-            for item in range(32):
-                big_a[item // 8, (item // 2) % 4, 2 * (item % 2) + z_low, half, :, cols] = (
-                    value[8 * item : 8 * item + 8]
-                )
+            value = (
+                dot(turned[0:512, :], m_hi[:, cols], NN)
+                + dot(turned[512:1024, :], m_hi[:, cols], NN)
+                + dot(turned[0:512, :], m_lo[:, cols], NN)
+            )
+            for item in range(64):
+                z = 2 * (item % 2) + item // 32
+                big_a[(item // 8) % 4, (item // 2) % 4, z, half, :, cols] = value[
+                    8 * item : 8 * item + 8
+                ]
             return 0
 
-        lax.fori_loop(0, 4, tile_grad, 0)
-
-    scatter_c.relay()
-    rotation_grad(0)
-    rotation_grad(1)
-    rotation_grad(2)
-    scatter_c.finish_ring()
-    scatter_c.start(1)
-    rotation_grad(3)
-    scatter_c.wait(1)
-    scatter_c.start(2)
-    scatter_c.wait(2)
-
-    g_high, g_low = split(factor * d_c[...] * total_c[mx, my, mz])
-    left = jnp.concatenate([c_high, c_high, c_low], axis=0)
-    right = jnp.concatenate([g_high, g_low, g_high], axis=0)
-    for group in range(4):
-        z_low, half = group // 2, group % 2
-        value = dot(left[:, 256 * group : 256 * group + 256], right, TN)
-        for item in range(32):
-            at = (item // 8, (item // 2) % 4, 2 * (item % 2) + z_low, half)
-            big_a[at] = big_a[at] + value[8 * item : 8 * item + 8]
+        lax.fori_loop(first, first + 2, tile_grad, 0)
 
     def pair_g(x):
         return remote(
@@ -525,18 +526,47 @@
             place.partner(),
         )
 
+    scatter_c.relay()
+    turn(1 - core)
+    rotation_grad(1 - core, 0)
+    rotation_grad(1 - core, 2)
     for x in range(RING):
         pair_g(x).start()
+    turn(core)
+    scatter_c.finish_ring()
+    scatter_c.start(1)
+    rotation_grad(core, 0)
+    rotation_grad(core, 2)
+    scatter_c.wait(1)
+    scatter_c.start(2)
     for x in range(RING):
         pair_g(x).wait()
-
-        def add(item, _):
-            at = (x, item // RING, item % RING)
-            total_g[at] = total_g[at] + big_a[(*at, core)]
-            return 0
-
-        lax.fori_loop(0, RING * RING, add, 0)
-    scatter_g = Scatter(place, total_g, lands_g, g_send, g_recv)
+    scatter_c.wait(2)
+
+    slopes[core] = factor * d_c[...] * total_c[mx, my, mz]
+    swap = remote(
+        slopes.at[core], slopes.at[core], swap_send.at[0], swap_recv.at[0], place.partner()
+    )
+    swap.start()
+    swap.wait()
+    g_high, g_low = split(slopes[...].reshape(32, -1))
+    c_right[...] = jnp.concatenate([g_high, g_low, g_high], axis=0)
+
+    def corpus_term(tile, _):
+        cols = pl.ds(pl.multiple_of(256 * tile, 256), 256)
+        for z_low in range(2):
+            value = dot(c_left[:, group_cols(z_low, core)], c_right[:, cols], TN)
+            for item in range(32):
+                at = (item // 8, (item // 2) % 4, 2 * (item % 2) + z_low)
+                total_g[(*at, slice(None), cols)] = (
+                    total_g[(*at, slice(None), cols)]
+                    + big_a[(*at, core, slice(None), cols)]
+                    + value[8 * item : 8 * item + 8]
+                )
+        return 0
+
+    lax.fori_loop(0, 4, corpus_term, 0)
+    scatter_g = Scatter(place, total_g, total_g, lands_g, g_send, g_recv)
     scatter_g.start_ring()
     scatter_g.relay()
     scatter_g.finish_ring()
@@ -551,9 +581,9 @@
     slots = teacher.shape[1]
     factor = 2.5 / math.sqrt(width)
 
-    def lands(depth, dtype):
+    def lands(depth, first_dtype):
         return [
-            pltpu.VMEM((RING - 1, *(RING,) * (2 - stage), depth, COLUMNS[colour][1]), dtype)
+            pltpu.VMEM((RING - 1, *(RING,) * (2 - stage), depth, COLUMNS[colour][1]), (first_dtype, F32, F32)[stage])
             for stage in range(3)
             for colour in range(COLOURS)
         ]
@@ -571,7 +601,7 @@
             pltpu.VMEM((4, 4, 4, 2, 8, width), F32),
             pltpu.VMEM((4, 4, 4, 2, 16, width), F32),
             pltpu.VMEM((rows, slots), BF16),
-            pltpu.VMEM((16, width), F32),
+            pltpu.VMEM((32, width), F32),
             pltpu.VMEM((width, width), BF16),
             pltpu.VMEM((width, width), BF16),
             pltpu.VMEM((rows, width), BF16),
@@ -585,8 +615,12 @@
             pltpu.VMEM((rows, 128), F32),
             pltpu.VMEM((4, 4, 4, 16, width), F32),
             pltpu.VMEM((4, 4, 4, 8, width), F32),
-            pltpu.VMEM((512, rows), BF16),
-            *lands(16, F32),
+            pltpu.VMEM((1024, rows), BF16),
+            pltpu.VMEM((4, 4, 4, 16, width), BF16),
+            pltpu.VMEM((2, 16, width), F32),
+            pltpu.VMEM((96, width), BF16),
+            pltpu.VMEM((96, width), BF16),
+            *lands(16, BF16),
             *lands(8, F32),
             dma((4,)),
             dma((54,)),
@@ -601,6 +635,8 @@
             dma((54,)),
             dma((4,)),
             dma((4,)),
+            dma((1,)),
+            dma((1,)),
         ],
         compiler_params=pltpu.CompilerParams(
             collective_id=0, has_side_effects=True, vmem_limit_bytes=67043328

time: 107 us -> 97.8 us (0.914)
  Pallas kernels: 105 us -> 96.2 us
    pallas_call x1, Pallas kernels: 105 us -> 96.2 us  [per_device(): pl.pallas_call(functools.partial(kernel, factor, slots // 2), out_shape=j...]
where the time goes in v3:
time: 97.8 us; the launch traced here: 97.6 us
  Pallas kernels  96.2 us (98%)
  local copies, waits for them, and re-layouts  1.38 us (1%)
    pallas_call x1, Pallas kernels, per_device(): pl.pallas_call(functools.partial(kernel, factor, slots // 2), out_shape=j...  96.2 us

profile of v3, /device:TPU:0, one launch (start us, length us, event | category | flops | bytes accessed | tf_op | source)
XLA Modules:
  0.0 97.6 jit_solution(11390927118776581930)
XLA Ops:
  0.0 96.2 %shard_map.73 = f32[8,1024]{1,0:T(8,128)} custom-call(f32[2,4,4,2,16,1024]{5,4,3,2,1,0:T(8,128)} %bitcast.4, f32[64,1024]{1,0:T(8,128)} %c_hbm.1, f32[4,4,4,2,8,1024]{5,4,3,2,1,0:T(8,128)} %bitcast.5, s32[32]{0:T(128)} %counts.1, bf16[1024,2048]{1,0:T(8,128)(2,1)} %t_hbm.1, f32[1,1024]{1,0:T(1,128)} %bitcast.6, f32[1,1024]{1,0:T(1,128)} %bitcast.7), custom_call_target="tpu_custom_call" | custom-call | tf_op jit(solution)/shard_map/pallas_call | solution.py:595
  96.2 1.4 %copy.9 = f32[8,1024]{1,0:T(8,128)} copy(f32[8,1024]{1,0:T(8,128)} %shard_map.73) | data formatting | bytes 65536

commit v4 on v3

--- a/solution.py
+++ b/solution.py
@@ -209,11 +209,15 @@
                 self.ring(colour, piece).wait()
             at = self.place.at[ORDERS[colour][0]]
             block, land = self.block(self.total, colour, at), self.lands[0][colour]
+            sent = self.block(self.sent, colour, at)
 
             def add(item, _):
                 inner = (item // RING, item % RING)
                 first, second = land[(0, *inner)], land[(1, *inner)]
-                block[inner] = block[inner] + first.astype(F32) + second.astype(F32)
+                value = block[inner] + first.astype(F32) + second.astype(F32)
+                block[inner] = value
+                if self.sent is not self.total:
+                    sent[inner] = value.astype(sent.dtype)
                 return 0
 
             lax.fori_loop(0, RING * RING, add, 0)
@@ -228,7 +232,7 @@
                     index[axis] = self.place.at[axis]
                 index[order[stage]], device = self.place.peer(order[stage], step)
                 yield remote(
-                    self.total.at[index[0], index[1], index[2], :, start : start + width],
+                    self.sent.at[index[0], index[1], index[2], :, start : start + width],
                     self.lands[stage][colour].at[step - 1],
                     self.send.at[slot],
                     self.recv.at[slot],
@@ -256,8 +260,11 @@
                     index[0], index[1], index[2], :, start : start + width
                 ]
                 for step in range(RING - 1):
-                    value = value + land[(step, *inner)]
-                self.total[index[0], index[1], index[2], :, start : start + width] = value
+                    value = value + land[(step, *inner)].astype(F32)
+                at = (index[0], index[1], index[2], slice(None), slice(start, start + width))
+                self.total[at] = value
+                if self.sent is not self.total:
+                    self.sent[at] = value.astype(self.sent.dtype)
                 return 0
 
             lax.fori_loop(0, RING ** len(rest), add, 0)
@@ -293,6 +300,7 @@
     total_g,
     turned,
     sent_c,
+    pair_land,
     slopes,
     c_left,
     c_right,
@@ -417,24 +425,39 @@
     shift_s[...] = jnp.broadcast_to(shift_s_ref[...], (128, 1024)).T
     shift_t[...] = jnp.broadcast_to(shift_t_ref[...], (128, 1024)).T
     load_t.wait()
-    gather.finish()
-
-    def weigh(item, _):
+
+    def place_of(item):
         block, half = item // 2, item % 2
         cols = pl.ds(pl.multiple_of(256 * block, 256), 256)
         rows = pl.ds(pl.multiple_of(512 * half, 512), 512)
-        part = codes[block // 2, pl.ds(2 * (block % 2), 2)].reshape(256, -1)
-        score = factor * dot(q_bits[rows, :], part, NT)
-        down_s, down_t = shift_s[rows, :], shift_t[rows, :]
-        student = jnp.exp(score - jnp.concatenate([down_s, down_s], axis=1))
-        target = jnp.exp(
-            t_buf[rows, cols].astype(F32) - jnp.concatenate([down_t, down_t], axis=1)
-        )
+        inner = pl.ds(pl.multiple_of(256 * (block % 4), 256), 256)
+        held = big_b.at[2 * (block // 4) + half, :, :, :, :, inner]
         lane = lax.broadcasted_iota(jnp.int32, (1, 256), 1)
         limit = jnp.zeros((1, 256), jnp.int32)
         for slot in range(4):
             limit = jnp.where(lane // 64 == slot, counts[4 * block + slot], limit)
         live = jnp.where(lane % 64 < limit, 1.0 / live_total, 0.0)
+        return block, rows, cols, held, live
+
+    def teach(item, _):
+        _, rows, cols, held, _ = place_of(item)
+        down = shift_t[rows, :]
+        target = jnp.exp(
+            t_buf[rows, cols].astype(F32) - jnp.concatenate([down, down], axis=1)
+        )
+        held[...] = target.reshape(4, 4, 2, 16, 256)
+        return 0
+
+    lax.fori_loop(0, 16, teach, 0)
+    gather.finish()
+
+    def weigh(item, _):
+        block, rows, cols, held, live = place_of(item)
+        part = codes[block // 2, pl.ds(2 * (block % 2), 2)].reshape(256, -1)
+        score = factor * dot(q_bits[rows, :], part, NT)
+        down = shift_s[rows, :]
+        student = jnp.exp(score - jnp.concatenate([down, down], axis=1))
+        target = held[...].reshape(512, 256)
         weights[rows, cols] = (live * (student - target)).astype(BF16)
         return 0
 
@@ -442,8 +465,8 @@
 
     def pair_c(x):
         return remote(
-            big_b.at[x, :, :, 1 - core],
-            total_c.at[x],
+            sent_c.at[x],
+            pair_land.at[x],
             cp_send.at[x],
             cp_recv.at[x],
             place.partner(),
@@ -455,7 +478,10 @@
         def corpus_grad(tile, _):
             cols = pl.ds(pl.multiple_of(256 * tile, 256), 256)
             part = dot(turned[0:512, :], q_bits[:, cols], NN)
-            big_b[x, :, :, :, :, cols] = part.reshape(4, 4, 2, 16, 256)
+            part = part.reshape(4, 4, 2, 16, 256)
+            zero, one = part[:, :, 0], part[:, :, 1]
+            total_c[x, :, :, :, cols] = lax.select(core == 0, zero, one)
+            sent_c[x, :, :, :, cols] = lax.select(core == 0, one, zero).astype(BF16)
             return 0
 
         lax.fori_loop(0, 4, corpus_grad, 0)
@@ -464,7 +490,7 @@
     def own_c(x):
         def add(item, _):
             at = (x, item // RING, item % RING)
-            value = total_c[at] + big_b[(*at, core)]
+            value = total_c[at] + pair_land[at].astype(F32)
             total_c[at] = value
             sent_c[at] = value.astype(BF16)
             return 0
@@ -581,9 +607,9 @@
     slots = teacher.shape[1]
     factor = 2.5 / math.sqrt(width)
 
-    def lands(depth, first_dtype):
+    def lands(depth, dtype):
         return [
-            pltpu.VMEM((RING - 1, *(RING,) * (2 - stage), depth, COLUMNS[colour][1]), (first_dtype, F32, F32)[stage])
+            pltpu.VMEM((RING - 1, *(RING,) * (2 - stage), depth, COLUMNS[colour][1]), dtype)
             for stage in range(3)
             for colour in range(COLOURS)
         ]
@@ -616,6 +642,7 @@
             pltpu.VMEM((4, 4, 4, 16, width), F32),
             pltpu.VMEM((4, 4, 4, 8, width), F32),
             pltpu.VMEM((1024, rows), BF16),
+            pltpu.VMEM((4, 4, 4, 16, width), BF16),
             pltpu.VMEM((4, 4, 4, 16, width), BF16),
             pltpu.VMEM((2, 16, width), F32),
             pltpu.VMEM((96, width), BF16),

time: 97.8 us -> 95.7 us (0.979)
  Pallas kernels: 96.2 us -> 94.1 us
    pallas_call x1, Pallas kernels: 96.2 us -> 94.1 us  [per_device(): pl.pallas_call(functools.partial(kernel, factor, slots // 2), out_shape=j...]
where the time goes in v4:
time: 95.7 us; the launch traced here: 95.5 us
  Pallas kernels  94.1 us (98%)
  local copies, waits for them, and re-layouts  1.38 us (1%)
    pallas_call x1, Pallas kernels, per_device(): pl.pallas_call(functools.partial(kernel, factor, slots // 2), out_shape=j...  94.1 us

profile of v4, /device:TPU:0, one launch (start us, length us, event | category | flops | bytes accessed | tf_op | source)
XLA Modules:
  0.0 95.5 jit_solution(5256308820864760076)
XLA Ops:
  0.0 94.1 %shard_map.73 = f32[8,1024]{1,0:T(8,128)} custom-call(f32[2,4,4,2,16,1024]{5,4,3,2,1,0:T(8,128)} %bitcast.4, f32[64,1024]{1,0:T(8,128)} %c_hbm.1, f32[4,4,4,2,8,1024]{5,4,3,2,1,0:T(8,128)} %bitcast.5, s32[32]{0:T(128)} %counts.1, bf16[1024,2048]{1,0:T(8,128)(2,1)} %t_hbm.1, f32[1,1024]{1,0:T(1,128)} %bitcast.6, f32[1,1024]{1,0:T(1,128)} %bitcast.7), custom_call_target="tpu_custom_call" | custom-call | tf_op jit(solution)/shard_map/pallas_call | solution.py:621
  94.2 1.4 %copy.9 = f32[8,1024]{1,0:T(8,128)} copy(f32[8,1024]{1,0:T(8,128)} %shard_map.73) | data formatting | bytes 65536
